TPU v7x, 32 devices: a whole 2x2x4 slice. The times are simulated.
32 devices in a mesh: jpair: 2 (over x), blk: 16 (over z, y, core).
Axes of the slice: x: 2, y: 2, z: 4, core: 2. Of those that a mesh axis runs over, the one named last changes fastest.
Arguments:
- dipole: bfloat16 [256, 12, 3, 256, 256], P('blk'), may hold values from -24 to 24
- block_cols: int32 [256, 12], P('blk'), may hold values from 0 to 255, as said below
- upper_vecs: bfloat16 [131072, 256], P(('jpair', 'blk')), parts along dimension 0, may hold values from -0.0234375 to 0.0234375
- lower_vecs: bfloat16 [131072, 128], P(('jpair', 'blk')), parts along dimension 0, may hold values from -0.0234375 to 0.0234375
- upper_energy: float32 [512], P('jpair'), parts along dimension 0, may hold values from 1 to 2
- lower_energy: float32 [256], P('jpair'), parts along dimension 0, may hold values from 0 to 0.8
Outputs:
- strength: float32 [512, 128], P(('jpair', 'blk')), parts along dimension 0
- intensity: float32 [512, 128], P(('jpair', 'blk')), parts along dimension 0
There are 2 independent parts, one for each index of `jpair`. A program takes and returns all parts, laid end to end along the dimension named above; an argument that names none is the same for every part. Nothing has to cross between parts.
Inputs may be any that keep to these rules, and one draw needn't show every extreme that they name: `block_cols`: within one block row the 12 block columns are distinct, and one of them is the row's own index. Splitting the block rows into 16 equal runs of consecutive rows, the columns of one run that fall in another run number at most 12 distinct blocks for each other run, and exactly 12 for some.
All inputs are finite; a program needn't handle non-finite values.
Results may differ from a plain program's by a relative error of at most 0.0026.
Values may be sent and summed in bfloat16 or wider, within the bound.
A program may use at most 256 MiB of HBM per device.

v0:
```python
import jax
import jax.numpy as jnp
from jax import lax
from jax.sharding import PartitionSpec as P

THERMAL = 0.3


def per_device(dipole, block_cols, upper_vecs, lower_vecs, upper_energy, lower_energy):
    rows_blk, nonzero, n_comps, block_size, _ = dipole.shape
    upper_count = upper_vecs.shape[1]
    lower_count = lower_vecs.shape[1]
    upper_blocks = upper_vecs.reshape(rows_blk, block_size, upper_count)
    halves = jnp.einsum(
        "rkast,rsu->rkatu", dipole, upper_blocks, preferred_element_type=jnp.float32
    ).astype(jnp.bfloat16)
    entry_count = rows_blk * nonzero
    halves = halves.reshape(entry_count, n_comps, block_size, upper_count)
    columns = block_cols.reshape(entry_count)
    group_size = lax.axis_size("blk")
    my_index = lax.axis_index("blk")
    gathered = lax.all_gather(lower_vecs, "blk", axis=0, tiled=True)
    all_blocks = gathered.reshape(gathered.shape[0] // block_size, block_size, lower_count)
    lows = jnp.take(all_blocks, columns, axis=0)
    proj = jnp.einsum("eatu,etl->aul", halves, lows, preferred_element_type=jnp.float32)
    share_rows = upper_count // group_size
    first_row = my_index * share_rows
    summed = lax.psum(proj, "blk")
    own_share = lax.dynamic_slice_in_dim(summed, first_row, share_rows, 1)
    strength = jnp.sum(own_share * own_share, axis=0)
    energy_rows = lax.dynamic_slice_in_dim(upper_energy, first_row, share_rows, 0)
    wavenumber = energy_rows[:, None] - lower_energy[None, :]
    intensity = wavenumber**3 * jnp.exp(-lower_energy / THERMAL)[None, :] * strength
    return (strength, intensity)


def solution(mesh):
    placed = (
        P("blk", None, None, None, None),
        P("blk", None),
        P(("jpair", "blk"), None),
        P(("jpair", "blk"), None),
        P("jpair"),
        P("jpair"),
    )
    return jax.shard_map(
        per_device,
        mesh=mesh,
        in_specs=placed,
        out_specs=(P(("jpair", "blk"), None), P(("jpair", "blk"), None)),
        check_vma=False,
    )
```

profile of v0, /device:TPU:0, one launch (start us, length us, event | category | flops | bytes accessed | tf_op | source)
XLA Modules:
  0.0 283.5 jit_solution(16496702931421474902)
XLA Ops:
  7.2 0.0 copy-start
  7.2 0.0 all-gather.2.cloned.1.call-start
  7.2 0.7 all-gather.2.cloned.1.call-update
  7.9 0.0 all-reduce.2.cloned.1.call-start
  8.0 0.8 reshape.59
  8.8 0.8 reshape.57
  9.5 0.8 dynamic_slice.7
  10.3 0.0 copy-done
  10.3 59.0 %convolution_convert_fusion = bf16[16,12,3,256,256]{4,3,2,1,0:T(8,128)(2,1)} fusion(bf16[16,12,3,256,256]{4,3,2,1,0:T(8,128)(2,1)} %param.6, bf16[16,256,256,1,1]{2,1,4,3,0:T(8,128)(2,1)S(1)} %bitcast.20), kind=kOutput, calls=%fused_computation.1 | convolution fusion | flops 19365101568 | bytes 153092096 | tf_op jit(solution)/shard_map/rkast,rsu->rkatu/dot_general | solution.py:14
  69.4 70.4 %all-gather.2.cloned.1.call-done = bf16[65536,128]{1,0:T(8,128)(2,1)} async-done(((bf16[4096,128]{1,0:T(8,128)(2,1)}), bf16[65536,128]{1,0:T(8,128)(2,1)}) %all-gather.2.cloned.1.call-update) | async-done | bytes 16777232 | tf_op jit(solution)/shard_map/all_gather | solution.py:22
  139.8 13.9 %gather_fusion = bf16[192,256,128]{2,1,0:T(8,128)(2,1)} fusion(bf16[256,256,128]{2,1,0:T(8,128)(2,1)} %bitcast.21, s32[1024]{0:T(1024)S(1)} %pad_clamp_fusion), kind=kCustom, calls=%fused_computation | custom fusion | bytes 25166592 | tf_op jit(solution)/shard_map/jit(_take)/gather | solution.py:24
  153.7 0.0 copy-start.2
  153.8 32.8 %fusion.5 = f32[3,256,128]{2,1,0:T(8,128)} fusion(bf16[192,3,256,256]{3,2,1,0:T(8,128)(2,1)} %bitcast.3, bf16[192,256,128]{2,1,0:T(8,128)(2,1)} %gather_fusion, pred[192]{0:T(512)(128)(4,1)S(1)} %compare_and_fusion), kind=kOutput, calls=%fused_computation.7 | convolution fusion | flops 9669967872 | bytes 88473792 | tf_op jit(solution)/shard_map/eatu,etl->aul/dot_general | solution.py:25
  186.6 0.0 all-reduce.2.cloned.1.call-update
  186.6 0.0 copy-done.2
  186.6 88.6 %all-reduce.2.cloned.1.call-done = f32[3,256,128]{2,1,0:T(8,128)} async-done(((f32[3,256,128]{2,1,0:T(8,128)}), f32[3,256,128]{2,1,0:T(8,128)}) %all-reduce.2.cloned.1.call-update) | async-done | bytes 393232 | tf_op jit(solution)/shard_map/psum | solution.py:28
  275.2 0.7 multiply_reduce_fusion
  276.0 0.0 copy-start.1
  276.0 0.7 fusion.9
  276.7 0.0 copy-done.1
  (4 shorter events, 0.0 us)
Async XLA Ops:
  7.2 3.2 %copy-start = (bf16[4096,256]{1,0:T(8,128)(2,1)S(1)}, bf16[4096,256]{1,0:T(8,128)(2,1)}, u32[]{:S(2)}) copy-start(bf16[4096,256]{1,0:T(8,128)(2,1)} %param.8) | copy-start | bytes 6291460
  7.2 132.6 %all-gather.2.cloned.1.call-start = ((), (), s32[]{:S(2)}) async-start(), calls=%async_computation | async-start | bytes 17825792 | tf_op jit(solution)/shard_map/all_gather | solution.py:22
  7.9 267.3 %all-reduce.2.cloned.1.call-start = ((), (), s32[]{:S(2)}) async-start(), calls=%async_computation.1 | async-start | bytes 786432 | tf_op jit(solution)/shard_map/psum | solution.py:28
  153.7 32.8 %copy-start.2 = (f32[128]{0:T(128)S(1)}, f32[128]{0:T(128)}, u32[]{:S(2)}) copy-start(f32[128]{0:T(128)} %param.11) | copy-start | bytes 1540
  276.0 0.7 copy-start.1
Sparse Core Ops, SparseCore 0:
  10.2 129.5 all-gather.1
  186.7 88.4 all-reduce.1
where the time goes:
time: 284 us; the launch traced here: 283 us
  waiting for transfers between devices  160 us (56%)
  matrix products  91.9 us (32%)
  local copies, waits for them, and re-layouts  16.3 us (6%)
  between operations  14.1 us (5%)
    psum x1, waiting for transfers between devices, per_device(): summed = lax.psum(proj, 'blk')  88.6 us
    all_gather x1, waiting for transfers between devices, per_device(): gathered = lax.all_gather(lower_vecs, 'blk', axis=0, tiled=True)  70.4 us
    dot_general x1, matrix products, per_device(): jnp.einsum('rkast,rsu->rkatu', dipole, upper_blocks, preferred_element_ty...  59 us
    dot_general x1, matrix products, per_device(): jnp.einsum('eatu,etl->aul', halves, lows, preferred_element_type=jnp.floa...  32.8 us
    gather x1, local copies, waits for them, and re-layouts, per_device(): lows = jnp.take(all_blocks, columns, axis=0)  13.9 us
  transfers between devices with their start and end apart: 2, of which 2 were waited for; matrix products, arithmetic and copies ran while one was open for 22% of the time, Pallas kernels for 0%

commit v1 on v0

--- a/solution.py
+++ b/solution.py
@@ -1,9 +1,39 @@
+import functools
 import jax
 import jax.numpy as jnp
 from jax import lax
 from jax.sharding import PartitionSpec as P
 
 THERMAL = 0.3
+
+
+def zone_begin(buf, where_dim):
+    right_arr = list(buf.shape[1:])
+    right_arr[where_dim] *= buf.shape[0]
+    m_next = jnp.moveaxis(buf, 0, where_dim).reshape(right_arr)
+    return m_next
+
+
+def search_bars(mat, peer_axis, k_dim):
+    world = lax.axis_size(peer_axis)
+    by_rank = [(p, (p + 1) % world) for p in range(world)]
+    mid_arr, r2 = ([], [])
+    pile = [(at, d) for d, at in by_rank]
+    for to_i in range(world - 1):
+        if to_i % 2 == 0:
+            mid_arr.append(
+                lax.ppermute(mid_arr[-1] if mid_arr else mat, axis_name=peer_axis, perm=by_rank)
+            )
+        else:
+            r2.append(lax.ppermute(r2[-1] if r2 else mat, axis_name=peer_axis, perm=pile))
+    tmp = jnp.stack([*mid_arr[::-1], mat, *r2], 0)
+    answer = lax.axis_index(peer_axis) - len(mid_arr)
+    tmp = tmp[(jnp.arange(world) - answer) % world]
+    reached = zone_begin(tmp, k_dim)
+    return reached
+
+
+turn_loops = functools.partial(search_bars, peer_axis="blk", k_dim=0)
 
 
 def per_device(dipole, block_cols, upper_vecs, lower_vecs, upper_energy, lower_energy):
@@ -19,7 +49,7 @@
     columns = block_cols.reshape(entry_count)
     group_size = lax.axis_size("blk")
     my_index = lax.axis_index("blk")
-    gathered = lax.all_gather(lower_vecs, "blk", axis=0, tiled=True)
+    gathered = turn_loops(lower_vecs)
     all_blocks = gathered.reshape(gathered.shape[0] // block_size, block_size, lower_count)
     lows = jnp.take(all_blocks, columns, axis=0)
     proj = jnp.einsum("eatu,etl->aul", halves, lows, preferred_element_type=jnp.float32)

time: 284 us -> 423 us (1.49)
  starting transfers between devices: 0.08 us -> 110 us
  local copies, waits for them, and re-layouts: 16.3 us -> 61.9 us
  waiting for transfers between devices: 160 us -> 144 us
    ppermute x0 -> x15, starting transfers between devices: none -> 110 us  [the longest x8 105 us: search_bars(): lax.ppermute(mid_arr[-1] if mid_arr else mat, axis_name=peer_axis, perm=b...]
    all_gather x1 -> x0, waiting for transfers between devices: 70.4 us -> none  [per_device(): gathered = lax.all_gather(lower_vecs, 'blk', axis=0, tiled=True)]
    ppermute x0 -> x15, waiting for transfers between devices: none -> 50.8 us  [the longest x8 50.8 us: search_bars(): lax.ppermute(mid_arr[-1] if mid_arr else mat, axis_name=peer_axis, perm=b...]
    unnamed x6 -> x55, local copies, waits for them, and re-layouts: 0.02 us -> 33.5 us
    gather x0 -> x1, local copies, waits for them, and re-layouts: none -> 13.1 us  [search_bars(): tmp = tmp[(jnp.arange(world) - answer) % world]]
    psum x1, waiting for transfers between devices: 88.6 us -> 93 us  [per_device(): summed = lax.psum(proj, 'blk')]
  transfers between devices with their start and end apart: 2 -> 16, of which waited for: 2 -> 8; matrix products, arithmetic and copies ran while one was open for 22% -> 21% of each run, Pallas kernels for 0% -> 0%
where the time goes in v1:
time: 423 us
  waiting for transfers between devices  144 us (34%)
  starting transfers between devices  110 us (26%)
  matrix products  90.9 us (21%)
  local copies, waits for them, and re-layouts  61.9 us (15%)
  between operations  14.2 us (3%)
    ppermute x8, starting transfers between devices, search_bars(): lax.ppermute(mid_arr[-1] if mid_arr else mat, axis_name=peer_axis, perm=b...  105 us
    psum x1, waiting for transfers between devices, per_device(): summed = lax.psum(proj, 'blk')  93 us
    dot_general x1, matrix products, per_device(): jnp.einsum('rkast,rsu->rkatu', dipole, upper_blocks, preferred_element_ty...  58.2 us
    ppermute x8, waiting for transfers between devices, search_bars(): lax.ppermute(mid_arr[-1] if mid_arr else mat, axis_name=peer_axis, perm=b...  50.8 us
    unnamed x55, local copies, waits for them, and re-layouts  33.5 us
    dot_general x1, matrix products, per_device(): jnp.einsum('eatu,etl->aul', halves, lows, preferred_element_type=jnp.floa...  32.7 us
    gather x1, local copies, waits for them, and re-layouts, per_device(): lows = jnp.take(all_blocks, columns, axis=0)  14 us
    gather x1, local copies, waits for them, and re-layouts, search_bars(): tmp = tmp[(jnp.arange(world) - answer) % world]  13.1 us
  transfers between devices with their start and end apart: 16, of which 8 were waited for; matrix products, arithmetic and copies ran while one was open for 21% of the time, Pallas kernels for 0%

profile of v1, /device:TPU:0, one launch (start us, length us, event | category | flops | bytes accessed | tf_op | source)
XLA Modules:
  0.0 422.6 jit_solution(9914563709074976912)
XLA Ops:
  7.2 0.0 copy-start
  7.2 0.0 all-reduce.2.cloned.1.call-start
  7.2 0.5 collective-permute-start
  7.7 17.7 %collective-permute-done = bf16[4096,128]{1,0:T(8,128)(2,1)S(1)} collective-permute-done((bf16[4096,128]{1,0:T(8,128)(2,1)}, bf16[4096,128]{1,0:T(8,128)(2,1)S(1)}, u32[]{:S(2)}, u32[]{:S(2)}) %collective-permute-start) | collective-permute-done | bytes 1048608 | tf_op jit(solution)/shard_map/ppermute | solution.py:25
  25.4 1.0 copy-done.2
  26.4 0.0 collective-permute-start.1
  26.4 4.4 %collective-permute-start.8 = (bf16[4096,128]{1,0:T(8,128)(2,1)}, bf16[4096,128]{1,0:T(8,128)(2,1)S(1)}, u32[]{:S(2)}, u32[]{:S(2)}) collective-permute-start(bf16[4096,128]{1,0:T(8,128)(2,1)} %param.9), channel_id=1, source_target_pairs={{1,0},{2,1},{3,2},{4,3},{5,4},{6,5},{7,6},{8,7},{9,8},{10,9},{11,1... | collective-permute-start | bytes 3145736 | tf_op jit(solution)/shard_map/ppermute | solution.py:28
  30.9 12.6 %collective-permute-done.1 = bf16[4096,128]{1,0:T(8,128)(2,1)S(1)} collective-permute-done((bf16[4096,128]{1,0:T(8,128)(2,1)S(1)}, bf16[4096,128]{1,0:T(8,128)(2,1)S(1)}, u32[]{:S(2)}, u32[]{:S(2)}) %collective-permute-start.1) | collective-permute-done | bytes 1048608 | tf_op jit(solution)/shard_map/ppermute | solution.py:25
  43.4 5.3 %collective-permute-start.2 = (bf16[4096,128]{1,0:T(8,128)(2,1)S(1)}, bf16[4096,128]{1,0:T(8,128)(2,1)S(1)}, u32[]{:S(2)}, u32[]{:S(2)}) collective-permute-start(bf16[4096,128]{1,0:T(8,128)(2,1)S(1)} %collective-permute-done.1), channel_id=1, source_target_pairs={{0,1},{1,2},{2,3},{3,4},{4,5},{5,6},{6,7},{7,8},{8,9},{9,10},{10,1... | collective-permute-start | bytes 3145736 | tf_op jit(solution)/shard_map/ppermute | solution.py:25
  48.8 0.0 collective-permute-done.8
  48.8 1.0 copy-done.3
  49.8 0.0 collective-permute-start.9
  49.8 10.7 %collective-permute-done.2 = bf16[4096,128]{1,0:T(8,128)(2,1)S(1)} collective-permute-done((bf16[4096,128]{1,0:T(8,128)(2,1)S(1)}, bf16[4096,128]{1,0:T(8,128)(2,1)S(1)}, u32[]{:S(2)}, u32[]{:S(2)}) %collective-permute-start.2) | collective-permute-done | bytes 1048608 | tf_op jit(solution)/shard_map/ppermute | solution.py:25
  60.5 13.8 %collective-permute-start.3 = (bf16[4096,128]{1,0:T(8,128)(2,1)S(1)}, bf16[4096,128]{1,0:T(8,128)(2,1)S(1)}, u32[]{:S(2)}, u32[]{:S(2)}) collective-permute-start(bf16[4096,128]{1,0:T(8,128)(2,1)S(1)} %collective-permute-done.2), channel_id=1, source_target_pairs={{0,1},{1,2},{2,3},{3,4},{4,5},{5,6},{6,7},{7,8},{8,9},{9,10},{10,1... | collective-permute-start | bytes 3145736 | tf_op jit(solution)/shard_map/ppermute | solution.py:25
  74.2 0.0 collective-permute-done.9
  74.2 0.1 collective-permute-start.10
  74.3 1.0 copy-done.6
  75.3 3.8 collective-permute-done.3
  79.1 19.9 %collective-permute-start.4 = (bf16[4096,128]{1,0:T(8,128)(2,1)S(1)}, bf16[4096,128]{1,0:T(8,128)(2,1)S(1)}, u32[]{:S(2)}, u32[]{:S(2)}) collective-permute-start(bf16[4096,128]{1,0:T(8,128)(2,1)S(1)} %collective-permute-done.3), channel_id=1, source_target_pairs={{0,1},{1,2},{2,3},{3,4},{4,5},{5,6},{6,7},{7,8},{8,9},{9,10},{10,1... | collective-permute-start | bytes 3145736 | tf_op jit(solution)/shard_map/ppermute | solution.py:25
  99.0 0.0 collective-permute-done.10
  99.0 0.1 collective-permute-start.11
  99.0 0.9 copy-done.9
  100.0 2.4 collective-permute-done.4
  102.4 21.4 %collective-permute-start.5 = (bf16[4096,128]{1,0:T(8,128)(2,1)S(1)}, bf16[4096,128]{1,0:T(8,128)(2,1)S(1)}, u32[]{:S(2)}, u32[]{:S(2)}) collective-permute-start(bf16[4096,128]{1,0:T(8,128)(2,1)S(1)} %collective-permute-done.4), channel_id=1, source_target_pairs={{0,1},{1,2},{2,3},{3,4},{4,5},{5,6},{6,7},{7,8},{8,9},{9,10},{10,1... | collective-permute-start | bytes 3145736 | tf_op jit(solution)/shard_map/ppermute | solution.py:25
  123.7 0.0 collective-permute-done.11
  123.7 1.0 copy-done.11
  124.7 0.0 collective-permute-start.12
  124.7 1.3 collective-permute-done.5
  126.0 22.3 %collective-permute-start.6 = (bf16[4096,128]{1,0:T(8,128)(2,1)S(1)}, bf16[4096,128]{1,0:T(8,128)(2,1)}, u32[]{:S(2)}, u32[]{:S(2)}) collective-permute-start(bf16[4096,128]{1,0:T(8,128)(2,1)S(1)} %collective-permute-done.5), channel_id=1, source_target_pairs={{0,1},{1,2},{2,3},{3,4},{4,5},{5,6},{6,7},{7,8},{8,9},{9,10},{10,1... | collective-permute-start | bytes 3145736 | tf_op jit(solution)/shard_map/ppermute | solution.py:25
  148.3 0.0 collective-permute-done.12
  148.3 0.0 collective-permute-start.13
  148.3 2.4 collective-permute-done.6
  150.7 22.2 %collective-permute-start.7 = (bf16[4096,128]{1,0:T(8,128)(2,1)}, bf16[4096,128]{1,0:T(8,128)(2,1)}, u32[]{:S(2)}, u32[]{:S(2)}) collective-permute-start(bf16[4096,128]{1,0:T(8,128)(2,1)} %collective-permute-done.6), channel_id=1, source_target_pairs={{0,1},{1,2},{2,3},{3,4},{4,5},{5,6},{6,7},{7,8},{8,9},{9,10},{10,1... | collective-permute-start | bytes 3145736 | tf_op jit(solution)/shard_map/ppermute | solution.py:25
  173.0 58.2 %convolution_convert_fusion = bf16[16,12,3,256,256]{4,3,2,1,0:T(8,128)(2,1)} fusion(bf16[16,12,3,256,256]{4,3,2,1,0:T(8,128)(2,1)} %param.6, bf16[16,256,256,1,1]{2,1,4,3,0:T(8,128)(2,1)S(1)} %bitcast.54), kind=kOutput, calls=%fused_computation.2 | convolution fusion | flops 19365101568 | bytes 153092096 | tf_op jit(solution)/shard_map/rkast,rsu->rkatu/dot_general | solution.py:44
  231.2 0.1 reshape.104
  231.3 0.1 reshape.103
  231.5 0.1 dynamic_slice.7
  231.6 0.0 collective-permute-done.13
  231.6 0.2 collective-permute-start.14
  231.9 0.0 collective-permute-done.7
  231.9 2.6 bitcast_dynamic-update-slice_fusion.15
  234.5 2.3 bitcast_dynamic-update-slice_fusion.14
  236.8 2.3 bitcast_dynamic-update-slice_fusion.13
  239.1 2.3 bitcast_dynamic-update-slice_fusion.12
  241.3 2.3 bitcast_dynamic-update-slice_fusion.11
  243.7 2.3 bitcast_dynamic-update-slice_fusion.10
  246.0 2.3 bitcast_dynamic-update-slice_fusion.9
  248.2 2.3 bitcast_dynamic-update-slice_fusion.8
  250.5 1.1 bitcast_dynamic-update-slice_fusion.7
  251.6 1.1 bitcast_dynamic-update-slice_fusion.6
  252.7 1.0 bitcast_dynamic-update-slice_fusion.5
  253.7 1.1 bitcast_dynamic-update-slice_fusion.4
  254.8 1.0 bitcast_dynamic-update-slice_fusion.3
  255.8 2.3 bitcast_dynamic-update-slice_fusion.2
  258.1 2.3 bitcast_dynamic-update-slice_fusion.1
  260.4 0.0 collective-permute-done.14
  260.4 1.1 bitcast_dynamic-update-slice_fusion
  261.5 13.1 %gather_fusion = bf16[16,4096,128]{2,1,0:T(8,128)(2,1)} fusion(bf16[16,4096,128]{2,1,0:T(8,128)(2,1)} %bitcast_dynamic-update-slice_fusion, s32[1024]{0:T(1024)S(1)} %pad_clamp_fusion.1), kind=kCustom, calls=%fused_computation | custom fusion | bytes 33554496 | tf_op jit(solution)/shard_map/gather | solution.py:31
  274.6 14.0 %gather_fusion.1 = bf16[192,256,128]{2,1,0:T(8,128)(2,1)} fusion(bf16[256,256,128]{2,1,0:T(8,128)(2,1)} %bitcast.55, s32[1024]{0:T(1024)S(1)} %pad_clamp_fusion), kind=kCustom, calls=%fused_computation.1 | custom fusion | bytes 25166592 | tf_op jit(solution)/shard_map/jit(_take)/gather | solution.py:54
  288.6 32.7 %fusion.5 = f32[3,256,128]{2,1,0:T(8,128)} fusion(bf16[192,3,256,256]{3,2,1,0:T(8,128)(2,1)} %bitcast.3, bf16[192,256,128]{2,1,0:T(8,128)(2,1)} %gather_fusion.1, pred[192]{0:T(512)(128)(4,1)S(1)} %compare_and_fusion), kind=kOutput, calls=%fused_computation.8 | convolution fusion | flops 9669967872 | bytes 88473792 | tf_op jit(solution)/shard_map/eatu,etl->aul/dot_general | solution.py:55
  321.3 0.0 all-reduce.2.cloned.1.call-update
  321.3 93.0 %all-reduce.2.cloned.1.call-done = f32[3,256,128]{2,1,0:T(8,128)} async-done(((f32[3,256,128]{2,1,0:T(8,128)}), f32[3,256,128]{2,1,0:T(8,128)}) %all-reduce.2.cloned.1.call-update) | async-done | bytes 393232 | tf_op jit(solution)/shard_map/psum | solution.py:58
  414.3 0.7 multiply_reduce_fusion
  415.1 0.7 fusion.9
  (40 shorter events, 0.1 us)
Async XLA Ops:
  7.2 165.8 %copy-start = (bf16[4096,256]{1,0:T(8,128)(2,1)S(1)}, bf16[4096,256]{1,0:T(8,128)(2,1)}, u32[]{:S(2)}) copy-start(bf16[4096,256]{1,0:T(8,128)(2,1)} %param.8) | copy-start | bytes 6291460
  7.2 407.1 %all-reduce.2.cloned.1.call-start = ((), (), s32[]{:S(2)}) async-start(), calls=%async_computation | async-start | bytes 786432 | tf_op jit(solution)/shard_map/psum | solution.py:58
  7.2 18.2 %collective-permute-start = (bf16[4096,128]{1,0:T(8,128)(2,1)}, bf16[4096,128]{1,0:T(8,128)(2,1)S(1)}, u32[]{:S(2)}, u32[]{:S(2)}) collective-permute-start(bf16[4096,128]{1,0:T(8,128)(2,1)} %param.9), channel_id=1, source_target_pairs={{0,1},{1,2},{2,3},{3,4},{4,5},{5,6},{6,7},{7,8},{8,9},{9,10},{10,1... | collective-permute-start | bytes 3145736 | tf_op jit(solution)/shard_map/ppermute | solution.py:25
  25.4 1.0 copy-start.2
  26.4 17.0 %collective-permute-start.1 = (bf16[4096,128]{1,0:T(8,128)(2,1)S(1)}, bf16[4096,128]{1,0:T(8,128)(2,1)S(1)}, u32[]{:S(2)}, u32[]{:S(2)}) collective-permute-start(bf16[4096,128]{1,0:T(8,128)(2,1)S(1)} %collective-permute-done), channel_id=1, source_target_pairs={{0,1},{1,2},{2,3},{3,4},{4,5},{5,6},{6,7},{7,8},{8,9},{9,10},{10,1... | collective-permute-start | bytes 3145736 | tf_op jit(solution)/shard_map/ppermute | solution.py:25
  26.4 22.4 %collective-permute-start.8 = (bf16[4096,128]{1,0:T(8,128)(2,1)}, bf16[4096,128]{1,0:T(8,128)(2,1)S(1)}, u32[]{:S(2)}, u32[]{:S(2)}) collective-permute-start(bf16[4096,128]{1,0:T(8,128)(2,1)} %param.9), channel_id=1, source_target_pairs={{1,0},{2,1},{3,2},{4,3},{5,4},{6,5},{7,6},{8,7},{9,8},{10,9},{11,1... | collective-permute-start | bytes 3145736 | tf_op jit(solution)/shard_map/ppermute | solution.py:28
  43.4 30.8 %copy-start.5 = (bf16[4096,128]{1,0:T(8,128)(2,1)}, bf16[4096,128]{1,0:T(8,128)(2,1)S(1)}, u32[]{:S(2)}) copy-start(bf16[4096,128]{1,0:T(8,128)(2,1)S(1)} %collective-permute-done.1) | copy-start | bytes 3145732
  43.4 17.0 %collective-permute-start.2 = (bf16[4096,128]{1,0:T(8,128)(2,1)S(1)}, bf16[4096,128]{1,0:T(8,128)(2,1)S(1)}, u32[]{:S(2)}, u32[]{:S(2)}) collective-permute-start(bf16[4096,128]{1,0:T(8,128)(2,1)S(1)} %collective-permute-done.1), channel_id=1, source_target_pairs={{0,1},{1,2},{2,3},{3,4},{4,5},{5,6},{6,7},{7,8},{8,9},{9,10},{10,1... | collective-permute-start | bytes 3145736 | tf_op jit(solution)/shard_map/ppermute | solution.py:25
  48.8 1.0 copy-start.3
  49.8 24.5 %collective-permute-start.9 = (bf16[4096,128]{1,0:T(8,128)(2,1)S(1)}, bf16[4096,128]{1,0:T(8,128)(2,1)S(1)}, u32[]{:S(2)}, u32[]{:S(2)}) collective-permute-start(bf16[4096,128]{1,0:T(8,128)(2,1)S(1)} %collective-permute-done.8), channel_id=1, source_target_pairs={{1,0},{2,1},{3,2},{4,3},{5,4},{6,5},{7,6},{8,7},{9,8},{10,9},{11,1... | collective-permute-start | bytes 3145736 | tf_op jit(solution)/shard_map/ppermute | solution.py:28
  60.5 38.5 %copy-start.8 = (bf16[4096,128]{1,0:T(8,128)(2,1)}, bf16[4096,128]{1,0:T(8,128)(2,1)S(1)}, u32[]{:S(2)}) copy-start(bf16[4096,128]{1,0:T(8,128)(2,1)S(1)} %collective-permute-done.2) | copy-start | bytes 3145732
  60.5 18.6 %collective-permute-start.3 = (bf16[4096,128]{1,0:T(8,128)(2,1)S(1)}, bf16[4096,128]{1,0:T(8,128)(2,1)S(1)}, u32[]{:S(2)}, u32[]{:S(2)}) collective-permute-start(bf16[4096,128]{1,0:T(8,128)(2,1)S(1)} %collective-permute-done.2), channel_id=1, source_target_pairs={{0,1},{1,2},{2,3},{3,4},{4,5},{5,6},{6,7},{7,8},{8,9},{9,10},{10,1... | collective-permute-start | bytes 3145736 | tf_op jit(solution)/shard_map/ppermute | solution.py:25
  74.2 1.0 copy-start.6
  74.2 24.7 %collective-permute-start.10 = (bf16[4096,128]{1,0:T(8,128)(2,1)S(1)}, bf16[4096,128]{1,0:T(8,128)(2,1)S(1)}, u32[]{:S(2)}, u32[]{:S(2)}) collective-permute-start(bf16[4096,128]{1,0:T(8,128)(2,1)S(1)} %collective-permute-done.9), channel_id=1, source_target_pairs={{1,0},{2,1},{3,2},{4,3},{5,4},{6,5},{7,6},{8,7},{9,8},{10,9},{11,1... | collective-permute-start | bytes 3145736 | tf_op jit(solution)/shard_map/ppermute | solution.py:28
  79.0 69.3 %copy-start.13 = (bf16[4096,128]{1,0:T(8,128)(2,1)}, bf16[4096,128]{1,0:T(8,128)(2,1)S(1)}, u32[]{:S(2)}) copy-start(bf16[4096,128]{1,0:T(8,128)(2,1)S(1)} %collective-permute-done.3) | copy-start | bytes 3145732
  79.1 23.3 %collective-permute-start.4 = (bf16[4096,128]{1,0:T(8,128)(2,1)S(1)}, bf16[4096,128]{1,0:T(8,128)(2,1)S(1)}, u32[]{:S(2)}, u32[]{:S(2)}) collective-permute-start(bf16[4096,128]{1,0:T(8,128)(2,1)S(1)} %collective-permute-done.3), channel_id=1, source_target_pairs={{0,1},{1,2},{2,3},{3,4},{4,5},{5,6},{6,7},{7,8},{8,9},{9,10},{10,1... | collective-permute-start | bytes 3145736 | tf_op jit(solution)/shard_map/ppermute | solution.py:25
  99.0 1.0 copy-start.9
  99.0 24.7 %collective-permute-start.11 = (bf16[4096,128]{1,0:T(8,128)(2,1)S(1)}, bf16[4096,128]{1,0:T(8,128)(2,1)S(1)}, u32[]{:S(2)}, u32[]{:S(2)}) collective-permute-start(bf16[4096,128]{1,0:T(8,128)(2,1)S(1)} %collective-permute-done.10), channel_id=1, source_target_pairs={{1,0},{2,1},{3,2},{4,3},{5,4},{6,5},{7,6},{8,7},{9,8},{10,9},{11,1... | collective-permute-start | bytes 3145736 | tf_op jit(solution)/shard_map/ppermute | solution.py:28
  102.4 45.9 %copy-start.14 = (bf16[4096,128]{1,0:T(8,128)(2,1)}, bf16[4096,128]{1,0:T(8,128)(2,1)S(1)}, u32[]{:S(2)}) copy-start(bf16[4096,128]{1,0:T(8,128)(2,1)S(1)} %collective-permute-done.4) | copy-start | bytes 3145732
  102.4 23.6 %collective-permute-start.5 = (bf16[4096,128]{1,0:T(8,128)(2,1)S(1)}, bf16[4096,128]{1,0:T(8,128)(2,1)S(1)}, u32[]{:S(2)}, u32[]{:S(2)}) collective-permute-start(bf16[4096,128]{1,0:T(8,128)(2,1)S(1)} %collective-permute-done.4), channel_id=1, source_target_pairs={{0,1},{1,2},{2,3},{3,4},{4,5},{5,6},{6,7},{7,8},{8,9},{9,10},{10,1... | collective-permute-start | bytes 3145736 | tf_op jit(solution)/shard_map/ppermute | solution.py:25
  123.7 1.0 copy-start.11
  124.7 23.6 %collective-permute-start.12 = (bf16[4096,128]{1,0:T(8,128)(2,1)S(1)}, bf16[4096,128]{1,0:T(8,128)(2,1)}, u32[]{:S(2)}, u32[]{:S(2)}) collective-permute-start(bf16[4096,128]{1,0:T(8,128)(2,1)S(1)} %collective-permute-done.11), channel_id=1, source_target_pairs={{1,0},{2,1},{3,2},{4,3},{5,4},{6,5},{7,6},{8,7},{9,8},{10,9},{11,1... | collective-permute-start | bytes 3145736 | tf_op jit(solution)/shard_map/ppermute | solution.py:28
  126.0 24.7 %copy-start.15 = (bf16[4096,128]{1,0:T(8,128)(2,1)}, bf16[4096,128]{1,0:T(8,128)(2,1)S(1)}, u32[]{:S(2)}) copy-start(bf16[4096,128]{1,0:T(8,128)(2,1)S(1)} %collective-permute-done.5) | copy-start | bytes 3145732
  126.0 24.7 %collective-permute-start.6 = (bf16[4096,128]{1,0:T(8,128)(2,1)S(1)}, bf16[4096,128]{1,0:T(8,128)(2,1)}, u32[]{:S(2)}, u32[]{:S(2)}) collective-permute-start(bf16[4096,128]{1,0:T(8,128)(2,1)S(1)} %collective-permute-done.5), channel_id=1, source_target_pairs={{0,1},{1,2},{2,3},{3,4},{4,5},{5,6},{6,7},{7,8},{8,9},{9,10},{10,1... | collective-permute-start | bytes 3145736 | tf_op jit(solution)/shard_map/ppermute | solution.py:25
  148.3 83.3 %collective-permute-start.13 = (bf16[4096,128]{1,0:T(8,128)(2,1)}, bf16[4096,128]{1,0:T(8,128)(2,1)}, u32[]{:S(2)}, u32[]{:S(2)}) collective-permute-start(bf16[4096,128]{1,0:T(8,128)(2,1)} %collective-permute-done.12), channel_id=1, source_target_pairs={{1,0},{2,1},{3,2},{4,3},{5,4},{6,5},{7,6},{8,7},{9,8},{10,9},{11,1... | collective-permute-start | bytes 3145736 | tf_op jit(solution)/shard_map/ppermute | solution.py:28
  150.7 81.1 %collective-permute-start.7 = (bf16[4096,128]{1,0:T(8,128)(2,1)}, bf16[4096,128]{1,0:T(8,128)(2,1)}, u32[]{:S(2)}, u32[]{:S(2)}) collective-permute-start(bf16[4096,128]{1,0:T(8,128)(2,1)} %collective-permute-done.6), channel_id=1, source_target_pairs={{0,1},{1,2},{2,3},{3,4},{4,5},{5,6},{6,7},{7,8},{8,9},{9,10},{10,1... | collective-permute-start | bytes 3145736 | tf_op jit(solution)/shard_map/ppermute | solution.py:25
  173.0 58.2 %copy-start.16 = (s32[16,12]{1,0:T(8,128)S(1)}, s32[16,12]{1,0:T(8,128)}, u32[]{:S(2)}) copy-start(s32[16,12]{1,0:T(8,128)} %param.7) | copy-start | bytes 2308
  173.0 58.4 %copy-start.19 = (f32[256]{0:T(256)S(1)}, f32[256]{0:T(256)}, u32[]{:S(2)}) copy-start(f32[256]{0:T(256)} %param.10) | copy-start | bytes 3076
  231.2 19.3 %copy-start.1 = (bf16[4096,128]{1,0:T(8,128)(2,1)S(1)}, bf16[4096,128]{1,0:T(8,128)(2,1)}, u32[]{:S(2)}) copy-start(bf16[4096,128]{1,0:T(8,128)(2,1)} %param.9) | copy-start | bytes 3145732
  231.4 20.2 %copy-start.4 = (bf16[4096,128]{1,0:T(8,128)(2,1)S(1)}, bf16[4096,128]{1,0:T(8,128)(2,1)}, u32[]{:S(2)}) copy-start(bf16[4096,128]{1,0:T(8,128)(2,1)} %copy-done.3) | copy-start | bytes 3145732
  231.4 21.3 %copy-start.7 = (bf16[4096,128]{1,0:T(8,128)(2,1)S(1)}, bf16[4096,128]{1,0:T(8,128)(2,1)}, u32[]{:S(2)}) copy-start(bf16[4096,128]{1,0:T(8,128)(2,1)} %copy-done.6) | copy-start | bytes 3145732
  231.4 22.3 %copy-start.10 = (bf16[4096,128]{1,0:T(8,128)(2,1)S(1)}, bf16[4096,128]{1,0:T(8,128)(2,1)}, u32[]{:S(2)}) copy-start(bf16[4096,128]{1,0:T(8,128)(2,1)} %copy-done.9) | copy-start | bytes 3145732
  231.4 23.3 %copy-start.12 = (bf16[4096,128]{1,0:T(8,128)(2,1)S(1)}, bf16[4096,128]{1,0:T(8,128)(2,1)}, u32[]{:S(2)}) copy-start(bf16[4096,128]{1,0:T(8,128)(2,1)} %copy-done.11) | copy-start | bytes 3145732
  231.6 28.8 %collective-permute-start.14 = (bf16[4096,128]{1,0:T(8,128)(2,1)}, bf16[4096,128]{1,0:T(8,128)(2,1)S(1)}, u32[]{:S(2)}, u32[]{:S(2)}) collective-permute-start(bf16[4096,128]{1,0:T(8,128)(2,1)} %collective-permute-done.13), channel_id=1, source_target_pairs={{1,0},{2,1},{3,2},{4,3},{5,4},{6,5},{7,6},{8,7},{9,8},{10,9},{11,1... | collective-permute-start | bytes 3145736 | tf_op jit(solution)/shard_map/ppermute | solution.py:28
  288.6 32.7 %copy-start.18 = (f32[128]{0:T(128)S(1)}, f32[128]{0:T(128)}, u32[]{:S(2)}) copy-start(f32[128]{0:T(128)} %param.11) | copy-start | bytes 1540
  415.1 0.7 copy-start.17
Sparse Core Ops, SparseCore 0:
  321.4 92.8 all-reduce.1
